TPU v7x, 32 devices: a whole 2x2x4 slice. The times are simulated.
32 devices in a mesh: groups: 2 (over y), zone: 4 (over x, core), tile: 4 (over z).
Axes of the slice: x: 2, y: 2, z: 4, core: 2. Of those that a mesh axis runs over, the one named last changes fastest.
Arguments:
- backscatter: bfloat16 [8, 2, 256, 512], P(('groups', 'zone'), None, 'tile'), parts along dimension 0, may hold values from -6 to 6
- row_bank: bfloat16 [16, 128, 128], replicated, may hold values from -0.3125 to 0.3125
- row_index: int32 [8, 4, 3], P(('groups', 'zone')), parts along dimension 0, may hold values from 0 to 3
- row_pick: int32 [8, 4, 3], P(('groups', 'zone')), parts along dimension 0, may hold values from 0 to 15
- row_mask: int32 [8, 4, 3], P(('groups', 'zone')), parts along dimension 0, may hold values 0 or 1
- column_bank: bfloat16 [16, 128, 128], replicated, may hold values from -0.3125 to 0.3125
- column_index: int32 [8, 2, 3], P(('groups', 'zone')), parts along dimension 0, may hold values from 0 to 1
- column_pick: int32 [8, 2, 3], P(('groups', 'zone')), parts along dimension 0, may hold values from 0 to 15
- column_mask: int32 [8, 2, 3], P(('groups', 'zone')), parts along dimension 0, may hold values 0 or 1
Outputs:
- geocoded: bfloat16 [8, 2, 256, 512], P(('groups', 'zone'), None, None, 'tile'), parts along dimension 0
There are 2 independent parts, one for each index of `groups`. A program takes and returns all parts, laid end to end along the dimension named above; an argument that names none is the same for every part. Nothing has to cross between parts.
All inputs are finite; a program needn't handle non-finite values. No bound on the sum of `row_mask` or of `column_mask` on one device may be relied on, other than what follows from the above.
Results may differ from a plain program's by a relative error of at most 0.0049.
Values may be sent and summed in bfloat16 or wider, within the bound.
No kernel may reach another device: no remote copies, remote signals or barrier semaphores. Data moves between devices by JAX's collectives and lax.ppermute only.
A program may use at most 64 MiB of HBM per device.

v0:
```python
import jax
import jax.numpy as jnp
from jax import lax
from jax.sharding import PartitionSpec as P

BLOCK = 128
EDGE = 64


def passed_along(block, axis, distance):
    devices = range(lax.axis_size(axis))
    route = [(i - distance, i) for i in devices if i - distance in devices]
    return lax.ppermute(block, axis, route)


def swap_panels(top_panel, bottom_panel):
    from_below = passed_along(top_panel, "zone", -1)
    from_above = passed_along(bottom_panel, "zone", 1)
    zone_index = lax.axis_index("zone")
    last_zone = lax.axis_size("zone") - 1
    feather = ((jnp.arange(EDGE, dtype=jnp.float32) + 0.5) / EDGE)[:, None]
    lower_blend = (
        (1.0 - feather) * bottom_panel.astype(jnp.float32)
        + feather * from_below.astype(jnp.float32)
    ).astype(jnp.bfloat16)
    upper_blend = (
        (1.0 - feather) * from_above.astype(jnp.float32) + feather * top_panel.astype(jnp.float32)
    ).astype(jnp.bfloat16)
    new_bottom = jnp.where(zone_index < last_zone, lower_blend, bottom_panel)
    new_top = jnp.where(zone_index > 0, upper_blend, top_panel)
    return (new_top, new_bottom)


def on_device(
    backscatter,
    row_bank,
    row_index,
    row_pick,
    row_mask,
    column_bank,
    column_index,
    column_pick,
    column_mask,
):
    image = backscatter[0]
    channels, lin_dev, samples = image.shape
    column_blocks = samples // BLOCK
    blocks = image.reshape(channels, lin_dev, column_blocks, BLOCK)
    gathered = blocks[:, :, row_index[0], :]
    row_weights = row_bank[row_pick[0]] * row_mask[0].astype(jnp.bfloat16)[:, :, None, None]
    along_samples = jnp.einsum(
        "clqbi,qbij->clqj", gathered, row_weights, preferred_element_type=jnp.float32
    )
    along_samples = along_samples.astype(jnp.bfloat16).reshape(channels, lin_dev, samples)
    line_blocks = column_index.shape[1]
    rows = line_blocks * BLOCK
    column_weights = (
        column_bank[column_pick[0]] * column_mask[0].astype(jnp.bfloat16)[:, :, None, None]
    )
    band_table = column_index[0]
    every_id = jnp.arange(line_blocks, dtype=jnp.int32)
    moved = lax.all_to_all(along_samples, "tile", split_axis=2, concat_axis=1, tiled=True)
    count = moved.shape[0]
    line_tiles = moved.reshape(count, line_blocks, BLOCK, BLOCK)
    picked = line_tiles[:, band_table[every_id]]
    result = jnp.einsum(
        "crbik,rboi->crok", picked, column_weights[every_id], preferred_element_type=jnp.float32
    )
    result = result.astype(jnp.bfloat16).reshape(count, every_id.shape[0] * BLOCK, BLOCK)
    new_top, new_bottom = swap_panels(result[:, :EDGE], result[:, rows - EDGE :])
    gridded = jnp.concatenate([new_top, result[:, EDGE : rows - EDGE], new_bottom], axis=1)
    return gridded[None]


def solution(mesh):
    in_specs = (
        P(("groups", "zone"), None, "tile", None),
        P(),
        P(("groups", "zone"), None, None),
        P(("groups", "zone"), None, None),
        P(("groups", "zone"), None, None),
        P(),
        P(("groups", "zone"), None, None),
        P(("groups", "zone"), None, None),
        P(("groups", "zone"), None, None),
    )
    out_specs = P(("groups", "zone"), None, None, "tile")
    return jax.shard_map(
        on_device, mesh=mesh, in_specs=in_specs, out_specs=out_specs, check_vma=False
    )
```

profile of v0, /device:TPU:1, one launch (start us, length us, event | category | flops | bytes accessed | tf_op | source)
XLA Modules:
  0.0 29.0 jit_solution(11059921443978826120)
XLA Ops:
  0.0 0.0 copy-start
  0.0 1.0 %reshape_squeeze.3 = bf16[2,64,4,128]{3,2,1,0:T(4,128)(2,1)S(1)} reshape(bf16[1,2,64,512]{3,2,1,0:T(8,128)(2,1)} %param.9) | data formatting | bytes 262144 | tf_op jit(solution)/shard_map/reshape;squeeze | solution.py:48
  1.0 0.0 copy-start.2
  1.0 0.6 %copy-done.2 = s32[1,4,3]{1,0,2:T(1,128)S(1)} copy-done((s32[1,4,3]{1,0,2:T(1,128)S(1)}, s32[1,4,3]{1,0,2:T(1,128)}, u32[]{:S(2)}) %copy-start.2) | copy-done | bytes 72
  1.7 0.1 copy.41
  1.8 0.1 reshape.158
  1.9 0.0 copy-start.3
  1.9 0.7 %copy-done.3 = s32[1,4,3]{1,0,2:T(1,128)S(1)} copy-done((s32[1,4,3]{1,0,2:T(1,128)S(1)}, s32[1,4,3]{1,0,2:T(1,128)}, u32[]{:S(2)}) %copy-start.3) | copy-done | bytes 72
  2.6 0.1 copy.39
  2.7 0.1 reshape.150
  2.7 0.0 copy-start.4
  2.8 0.7 %copy-done.4 = s32[1,4,3]{1,0,2:T(1,128)S(1)} copy-done((s32[1,4,3]{1,0,2:T(1,128)S(1)}, s32[1,4,3]{1,0,2:T(1,128)}, u32[]{:S(2)}) %copy-start.4) | copy-done | bytes 72
  3.4 0.1 copy.40
  3.5 0.6 %gather_fusion.3 = bf16[12,2,64,128]{3,2,1,0:T(8,128)(2,1)S(1)} fusion(bf16[2,64,4,128]{3,1,2,0:T(8,128)(2,1)S(1)} %copy.42, s32[1024]{0:T(1024)S(1)} %pad_clamp_fusion.1), kind=kCustom, calls=%fused_computation.3 | custom fusion | bytes 786480 | tf_op jit(solution)/shard_map/gather | solution.py:49
  4.2 0.0 copy-done
  4.2 0.6 %gather_fusion.2 = bf16[12,128,128]{2,1,0:T(8,128)(2,1)S(1)} fusion(bf16[16,128,128]{2,1,0:T(8,128)(2,1)S(1)} %copy-done, s32[1024]{0:T(1024)S(1)} %pad_clamp_fusion.2), kind=kCustom, calls=%fused_computation.2 | custom fusion | bytes 786480 | tf_op jit(solution)/shard_map/gather | solution.py:50
  4.8 0.3 %fusion.2 = bf16[2,64,4,128]{3,1,0,2:T(8,128)(2,1)S(1)} fusion(bf16[2,64,4,3,128]{4,1,0,3,2:T(8,128)(2,1)S(1)} %bitcast.85, bf16[4,3,128,128]{3,2,1,0:T(8,128)(2,1)S(1)} %bitcast.87, bf16[4,3]{1,0:T(4,128)(2,1)S(1)} %bitcast.89), kind=kOutput, calls=%fused_computation.10 | convolution fusion | flops 51183616 | bytes 917528 | tf_op jit(solution)/shard_map/clqbi,qbij->clqj/dot_general | solution.py:51
  5.2 0.2 copy.54
  5.3 0.9 %reshape.188 = bf16[4,2,8192]{2,1,0:T(2,128)(2,1)} reshape(bf16[512,2,64]{2,1,0:T(2,128)(2,1)S(1)} %bitcast.79) | data formatting | bytes 262144
  6.2 5.4 %all-to-all-start = ((bf16[4,2,8192]{2,1,0:T(2,128)(2,1)}), bf16[4,2,8192]{2,1,0:T(2,128)(2,1)S(1)}, u32[]{:S(2)}, u32[]{:S(2)}) async-start(bf16[4,2,8192]{2,1,0:T(2,128)(2,1)} %reshape.188), calls=%async_computation | async-start | bytes 262144 | tf_op jit(solution)/shard_map/all_to_all | solution.py:62
  11.6 0.0 copy-start.5
  11.7 0.7 %copy-done.5 = s32[1,2,3]{2,1,0:T(2,128)S(1)} copy-done((s32[1,2,3]{2,1,0:T(2,128)S(1)}, s32[1,2,3]{2,1,0:T(2,128)}, u32[]{:S(2)}) %copy-start.5) | copy-done | bytes 48
  12.3 0.1 reshape.134
  12.4 0.0 copy-start.6
  12.4 0.7 %copy-done.6 = s32[1,2,3]{2,1,0:T(2,128)S(1)} copy-done((s32[1,2,3]{2,1,0:T(2,128)S(1)}, s32[1,2,3]{2,1,0:T(2,128)}, u32[]{:S(2)}) %copy-start.6) | copy-done | bytes 48
  13.1 0.0 copy-start.1
  13.1 0.7 %copy-done.1 = s32[1,2,3]{2,1,0:T(2,128)S(1)} copy-done((s32[1,2,3]{2,1,0:T(2,128)S(1)}, s32[1,2,3]{2,1,0:T(2,128)}, u32[]{:S(2)}) %copy-start.1) | copy-done | bytes 48
  13.8 0.6 %gather_fusion.4 = s32[2,3]{1,0:T(2,128)S(1)} fusion(s32[2,3]{1,0:T(2,128)S(1)} %bitcast.88, s32[1024]{0:T(1024)S(1)} %pad_clamp_fusion.3), kind=kCustom, calls=%fused_computation.4 | custom fusion | bytes 56 | tf_op jit(solution)/shard_map/gather | solution.py:65
  14.3 1.6 %gather_fusion = bf16[6,128,128]{2,1,0:T(8,128)(2,1)S(1)} fusion(bf16[16,128,128]{2,1,0:T(8,128)(2,1)} %param.14, s32[1024]{0:T(1024)S(1)} %pad_clamp_fusion.4), kind=kCustom, calls=%fused_computation | custom fusion | bytes 393240 | tf_op jit(solution)/shard_map/gather | solution.py:58
  16.0 0.1 broadcast_multiply_fusion
  16.1 0.1 reshape.174
  16.1 0.6 %gather_fusion.1 = bf16[2,3,128,128]{3,2,1,0:T(8,128)(2,1)S(1)} fusion(bf16[2,3,128,128]{3,2,1,0:T(8,128)(2,1)S(1)} %broadcast_multiply_fusion, s32[1024]{0:T(1024)S(1)} %pad_clamp_fusion.3), kind=kCustom, calls=%fused_computation.1 | custom fusion | bytes 393224 | tf_op jit(solution)/shard_map/gather | solution.py:67
  16.8 0.0 all-to-all-done
  16.8 0.2 reshape.189
  17.0 0.2 copy.55
  17.2 0.6 %gather_fusion.5 = bf16[6,2,128,128]{3,2,1,0:T(8,128)(2,1)S(1)} fusion(bf16[2,2,128,128]{3,2,1,0:T(8,128)(2,1)S(1)} %bitcast.77, s32[1024]{0:T(1024)S(1)} %pad_clamp_fusion), kind=kCustom, calls=%fused_computation.5 | custom fusion | bytes 786456 | tf_op jit(solution)/shard_map/gather | solution.py:65
  17.8 0.2 fusion.3
  18.1 4.9 %collective-permute-start = (bf16[2,64,128]{2,1,0:T(8,128)(2,1)S(1)}, bf16[2,64,128]{2,1,0:T(8,128)(2,1)S(1)}, u32[]{:S(2)}, u32[]{:S(2)}) collective-permute-start(bf16[2,64,128]{2,1,0:T(8,128)(2,1)S(1)} %get-tuple-element.7), channel_id=1, source_target_pairs={{0,4},{4,8},{8,12},{1,5},{5,9},{9,13},{2,6},{6,10},{10,14},{3,7},{... | collective-permute-start | bytes 98312 | tf_op jit(solution)/shard_map/ppermute | solution.py:13
  23.0 1.9 %collective-permute-start.1 = (bf16[2,64,128]{2,1,0:T(8,128)(2,1)S(1)}, bf16[2,64,128]{2,1,0:T(8,128)(2,1)S(1)}, u32[]{:S(2)}, u32[]{:S(2)}) collective-permute-start(bf16[2,64,128]{2,1,0:T(8,128)(2,1)S(1)} %get-tuple-element.8), channel_id=1, source_target_pairs={{4,0},{8,4},{12,8},{5,1},{9,5},{13,9},{6,2},{10,6},{14,10},{7,3},{... | collective-permute-start | bytes 98312 | tf_op jit(solution)/shard_map/ppermute | solution.py:13
  25.0 0.0 collective-permute-done
  25.0 3.3 %collective-permute-done.1 = bf16[2,64,128]{2,1,0:T(8,128)(2,1)S(1)} collective-permute-done((bf16[2,64,128]{2,1,0:T(8,128)(2,1)S(1)}, bf16[2,64,128]{2,1,0:T(8,128)(2,1)S(1)}, u32[]{:S(2)}, u32[]{:S(2)}) %collective-permute-start.1) | collective-permute-done | bytes 32800 | tf_op jit(solution)/shard_map/ppermute | solution.py:13
  28.2 0.1 fusion.8
  28.3 0.7 %maximum_bitcast_fusion = bf16[1,2,256,128]{3,2,1,0:T(8,128)(2,1)} fusion(bf16[2,64,128]{2,1,0:T(8,128)(2,1)S(1)} %get-tuple-element.6, bf16[2,128,128]{2,1,0:T(8,128)(2,1)S(1)} %slice.26, bf16[2,64,128]{2,1,0:T(8,128)(2,1)S(1)} %get-tuple-element.5), kind=kLoop, calls=%fused_computation.16 | loop fusion | flops 393216 | bytes 262144 | tf_op jit(solution)/shard_map/broadcast_in_dim | solution.py:72
  (18 shorter events, 0.1 us)
Async XLA Ops:
  0.0 4.2 %copy-start = (bf16[16,128,128]{2,1,0:T(8,128)(2,1)S(1)}, bf16[16,128,128]{2,1,0:T(8,128)(2,1)}, u32[]{:S(2)}) copy-start(bf16[16,128,128]{2,1,0:T(8,128)(2,1)} %param.10) | copy-start | bytes 1572868
  1.0 0.7 %copy-start.2 = (s32[1,4,3]{1,0,2:T(1,128)S(1)}, s32[1,4,3]{1,0,2:T(1,128)}, u32[]{:S(2)}) copy-start(s32[1,4,3]{1,0,2:T(1,128)} %param.11) | copy-start | bytes 148
  1.9 0.7 %copy-start.3 = (s32[1,4,3]{1,0,2:T(1,128)S(1)}, s32[1,4,3]{1,0,2:T(1,128)}, u32[]{:S(2)}) copy-start(s32[1,4,3]{1,0,2:T(1,128)} %param.12) | copy-start | bytes 148
  2.7 0.7 %copy-start.4 = (s32[1,4,3]{1,0,2:T(1,128)S(1)}, s32[1,4,3]{1,0,2:T(1,128)}, u32[]{:S(2)}) copy-start(s32[1,4,3]{1,0,2:T(1,128)} %param.13) | copy-start | bytes 148
  6.2 10.5 %all-to-all-start = ((bf16[4,2,8192]{2,1,0:T(2,128)(2,1)}), bf16[4,2,8192]{2,1,0:T(2,128)(2,1)S(1)}, u32[]{:S(2)}, u32[]{:S(2)}) async-start(bf16[4,2,8192]{2,1,0:T(2,128)(2,1)} %reshape.188), calls=%async_computation | async-start | bytes 262144 | tf_op jit(solution)/shard_map/all_to_all | solution.py:62
  11.6 0.7 %copy-start.5 = (s32[1,2,3]{2,1,0:T(2,128)S(1)}, s32[1,2,3]{2,1,0:T(2,128)}, u32[]{:S(2)}) copy-start(s32[1,2,3]{2,1,0:T(2,128)} %param.16) | copy-start | bytes 76
  12.4 0.7 %copy-start.6 = (s32[1,2,3]{2,1,0:T(2,128)S(1)}, s32[1,2,3]{2,1,0:T(2,128)}, u32[]{:S(2)}) copy-start(s32[1,2,3]{2,1,0:T(2,128)} %param.17) | copy-start | bytes 76
  13.1 0.7 %copy-start.1 = (s32[1,2,3]{2,1,0:T(2,128)S(1)}, s32[1,2,3]{2,1,0:T(2,128)}, u32[]{:S(2)}) copy-start(s32[1,2,3]{2,1,0:T(2,128)} %param.15) | copy-start | bytes 76
  18.1 6.9 %collective-permute-start = (bf16[2,64,128]{2,1,0:T(8,128)(2,1)S(1)}, bf16[2,64,128]{2,1,0:T(8,128)(2,1)S(1)}, u32[]{:S(2)}, u32[]{:S(2)}) collective-permute-start(bf16[2,64,128]{2,1,0:T(8,128)(2,1)S(1)} %get-tuple-element.7), channel_id=1, source_target_pairs={{0,4},{4,8},{8,12},{1,5},{5,9},{9,13},{2,6},{6,10},{10,14},{3,7},{... | collective-permute-start | bytes 98312 | tf_op jit(solution)/shard_map/ppermute | solution.py:13
  23.0 5.2 %collective-permute-start.1 = (bf16[2,64,128]{2,1,0:T(8,128)(2,1)S(1)}, bf16[2,64,128]{2,1,0:T(8,128)(2,1)S(1)}, u32[]{:S(2)}, u32[]{:S(2)}) collective-permute-start(bf16[2,64,128]{2,1,0:T(8,128)(2,1)S(1)} %get-tuple-element.8), channel_id=1, source_target_pairs={{4,0},{8,4},{12,8},{5,1},{9,5},{13,9},{6,2},{10,6},{14,10},{7,3},{... | collective-permute-start | bytes 98312 | tf_op jit(solution)/shard_map/ppermute | solution.py:13
where the time goes:
time: 29.4 us; the launch traced here: 29 us
  starting transfers between devices  12.2 us (41%)
  local copies, waits for them, and re-layouts  11.8 us (40%)
  waiting for transfers between devices  3.26 us (11%)
  other arithmetic  0.91 us (3%)
  matrix products  0.57 us (2%)
    ppermute x2, starting transfers between devices, passed_along(): return lax.ppermute(block, axis, route)  6.83 us
    all_to_all x1, starting transfers between devices, on_device(): lax.all_to_all(along_samples, 'tile', split_axis=2, concat_axis=1, tiled=...  5.41 us
    unnamed x16, local copies, waits for them, and re-layouts  5.14 us
    ppermute x2, waiting for transfers between devices, passed_along(): return lax.ppermute(block, axis, route)  3.26 us
    gather x1, local copies, waits for them, and re-layouts, on_device(): column_bank[column_pick[0]]  1.62 us
    gather x2, local copies, waits for them, and re-layouts, on_device(): picked = line_tiles[:, band_table[every_id]]  1.18 us
    another operation x2, local copies, waits for them, and re-layouts, on_device(): blocks = image.reshape(channels, lin_dev, column_blocks, BLOCK)  1.02 us
    broadcast_in_dim x1, other arithmetic, on_device(): return gridded[None]  0.67 us
  transfers between devices with their start and end apart: 3, of which 1 were waited for; matrix products, arithmetic and copies ran while one was open for 11% of the time, Pallas kernels for 0%

commit v1 on v0

--- a/solution.py
+++ b/solution.py
@@ -59,7 +59,19 @@
     )
     band_table = column_index[0]
     every_id = jnp.arange(line_blocks, dtype=jnp.int32)
-    moved = lax.all_to_all(along_samples, "tile", split_axis=2, concat_axis=1, tiled=True)
+    ways, here = (lax.axis_size("tile"), lax.axis_index("tile"))
+    width = along_samples.shape[2] // ways
+    shape = list(along_samples.shape)
+    shape[2] = width
+    height = shape[1]
+    shape[1] = height * ways
+    full = jnp.zeros(shape, along_samples.dtype)
+    for mask in range(ways):
+        part = lax.dynamic_slice_in_dim(along_samples, (here ^ mask) * width, width, axis=2)
+        if mask:
+            part = lax.ppermute(part, "tile", [(d, d ^ mask) for d in range(ways)])
+        full = lax.dynamic_update_slice_in_dim(full, part, (here ^ mask) * height, axis=1)
+    moved = full
     count = moved.shape[0]
     line_tiles = moved.reshape(count, line_blocks, BLOCK, BLOCK)
     picked = line_tiles[:, band_table[every_id]]

time: 29.4 us -> 26.3 us (0.89)
  local copies, waits for them, and re-layouts: 11.8 us -> 9.24 us
  starting transfers between devices: 12.2 us -> 11.7 us
    all_to_all x1 -> x0, starting transfers between devices: 5.41 us -> none  [on_device(): lax.all_to_all(along_samples, 'tile', split_axis=2, concat_axis=1, tiled=...]
    ppermute x0 -> x3, starting transfers between devices: none -> 4.49 us  [on_device(): part = lax.ppermute(part, 'tile', [(d, d ^ mask) for d in range(ways)])]
    unnamed x16 -> x14, local copies, waits for them, and re-layouts: 5.14 us -> 2.8 us
    ppermute x2, starting transfers between devices: 6.83 us -> 7.2 us  [passed_along(): return lax.ppermute(block, axis, route)]
  transfers between devices with their start and end apart: 3 -> 5, of which waited for: 1 -> 1; matrix products, arithmetic and copies ran while one was open for 11% -> 12% of each run, Pallas kernels for 0% -> 0%
where the time goes in v1:
time: 26.3 us; the launch traced here: 26 us
  starting transfers between devices  11.7 us (44%)
  local copies, waits for them, and re-layouts  9.24 us (35%)
  waiting for transfers between devices  3.28 us (12%)
  other arithmetic  0.91 us (3%)
  matrix products  0.56 us (2%)
  between operations  0.29 us (1%)
    ppermute x2, starting transfers between devices, passed_along(): return lax.ppermute(block, axis, route)  7.2 us
    ppermute x3, starting transfers between devices, on_device(): part = lax.ppermute(part, 'tile', [(d, d ^ mask) for d in range(ways)])  4.49 us
    ppermute x2, waiting for transfers between devices, passed_along(): return lax.ppermute(block, axis, route)  3.26 us
    unnamed x14, local copies, waits for them, and re-layouts  2.8 us
    gather x1, local copies, waits for them, and re-layouts, on_device(): column_bank[column_pick[0]]  1.62 us
    gather x2, local copies, waits for them, and re-layouts, on_device(): picked = line_tiles[:, band_table[every_id]]  1.18 us
    another operation x2, local copies, waits for them, and re-layouts, on_device(): blocks = image.reshape(channels, lin_dev, column_blocks, BLOCK)  1.02 us
    broadcast_in_dim x1, other arithmetic, on_device(): return gridded[None]  0.67 us
  transfers between devices with their start and end apart: 5, of which 1 were waited for; matrix products, arithmetic and copies ran while one was open for 12% of the time, Pallas kernels for 0%

profile of v1, /device:TPU:1, one launch (start us, length us, event | category | flops | bytes accessed | tf_op | source)
XLA Modules:
  0.0 26.0 jit_solution(1329208109903131483)
XLA Ops:
  0.0 0.0 copy-start
  0.0 1.0 %reshape_squeeze.3 = bf16[2,64,4,128]{3,2,1,0:T(4,128)(2,1)S(1)} reshape(bf16[1,2,64,512]{3,2,1,0:T(8,128)(2,1)} %param.9) | data formatting | bytes 262144 | tf_op jit(solution)/shard_map/reshape;squeeze | solution.py:48
  1.0 0.0 copy-start.3
  1.0 0.0 copy-start.4
  1.1 0.6 %copy-done.3 = s32[1,4,3]{1,0,2:T(1,128)S(1)} copy-done((s32[1,4,3]{1,0,2:T(1,128)S(1)}, s32[1,4,3]{1,0,2:T(1,128)}, u32[]{:S(2)}) %copy-start.3) | copy-done | bytes 72
  1.7 0.0 copy-done.4
  1.7 0.1 copy.22
  1.8 0.1 reshape.157
  1.9 0.1 copy.20
  2.0 0.1 reshape.149
  2.1 0.0 copy-start.2
  2.1 0.7 %copy-done.2 = s32[1,4,3]{1,0,2:T(1,128)S(1)} copy-done((s32[1,4,3]{1,0,2:T(1,128)S(1)}, s32[1,4,3]{1,0,2:T(1,128)}, u32[]{:S(2)}) %copy-start.2) | copy-done | bytes 72
  2.8 0.1 copy.21
  2.9 0.6 %gather_fusion.3 = bf16[12,2,64,128]{3,2,1,0:T(8,128)(2,1)S(1)} fusion(bf16[2,64,4,128]{3,1,2,0:T(8,128)(2,1)S(1)} %copy.23, s32[1024]{0:T(1024)S(1)} %pad_clamp_fusion.1), kind=kCustom, calls=%fused_computation.3 | custom fusion | bytes 786480 | tf_op jit(solution)/shard_map/gather | solution.py:49
  3.5 0.0 copy-done
  3.5 0.6 %gather_fusion.2 = bf16[12,128,128]{2,1,0:T(8,128)(2,1)S(1)} fusion(bf16[16,128,128]{2,1,0:T(8,128)(2,1)S(1)} %copy-done, s32[1024]{0:T(1024)S(1)} %pad_clamp_fusion.2), kind=kCustom, calls=%fused_computation.2 | custom fusion | bytes 786480 | tf_op jit(solution)/shard_map/gather | solution.py:50
  4.1 0.3 %fusion.2 = bf16[4,2,8,8,128]{4,3,2,1,0:T(8,128)(2,1)S(1)} fusion(bf16[2,64,4,3,128]{4,1,0,3,2:T(8,128)(2,1)S(1)} %bitcast.82, bf16[4,3,128,128]{3,2,1,0:T(8,128)(2,1)S(1)} %bitcast.84, bf16[4,3]{1,0:T(4,128)(2,1)S(1)} %bitcast.86), kind=kOutput, calls=%fused_computation.10 | convolution fusion | flops 51183616 | bytes 917528 | tf_op jit(solution)/shard_map/clqbi,qbij->clqj/dot_general | solution.py:51
  4.6 2.2 %collective-permute-start = (bf16[2,64,128]{2,1,0:T(8,128)(2,1)S(1)}, bf16[2,64,128]{2,1,0:T(8,128)(2,1)S(1)}, u32[]{:S(2)}, u32[]{:S(2)}) collective-permute-start(bf16[2,64,128]{2,1,0:T(8,128)(2,1)S(1)} %get-tuple-element.11), channel_id=1, source_target_pairs={{0,1},{1,0},{2,3},{3,2},{4,5},{5,4},{6,7},{7,6},{8,9},{9,8},{10,11... | collective-permute-start | bytes 98312 | tf_op jit(solution)/shard_map/ppermute | solution.py:72
  6.8 2.3 %collective-permute-start.1 = (bf16[2,64,128]{2,1,0:T(8,128)(2,1)S(1)}, bf16[2,64,128]{2,1,0:T(8,128)(2,1)S(1)}, u32[]{:S(2)}, u32[]{:S(2)}) collective-permute-start(bf16[2,64,128]{2,1,0:T(8,128)(2,1)S(1)} %get-tuple-element.10), channel_id=1, source_target_pairs={{0,2},{1,3},{2,0},{3,1},{4,6},{5,7},{6,4},{7,5},{8,10},{9,11},{10,... | collective-permute-start | bytes 98312 | tf_op jit(solution)/shard_map/ppermute | solution.py:72
  9.1 0.0 collective-permute-start.2
  9.1 0.0 copy-start.1
  9.1 0.7 %copy-done.1 = s32[1,2,3]{2,1,0:T(2,128)S(1)} copy-done((s32[1,2,3]{2,1,0:T(2,128)S(1)}, s32[1,2,3]{2,1,0:T(2,128)}, u32[]{:S(2)}) %copy-start.1) | copy-done | bytes 48
  9.8 0.0 copy-start.5
  9.8 0.6 %gather_fusion.4 = s32[2,3]{1,0:T(2,128)S(1)} fusion(s32[2,3]{1,0:T(2,128)S(1)} %bitcast.85, s32[1024]{0:T(1024)S(1)} %pad_clamp_fusion.3), kind=kCustom, calls=%fused_computation.4 | custom fusion | bytes 56 | tf_op jit(solution)/shard_map/gather | solution.py:77
  10.4 0.1 copy-done.5
  10.5 0.1 reshape.173
  10.6 0.1 reshape.133
  10.7 0.0 copy-start.6
  10.7 0.7 %copy-done.6 = s32[1,2,3]{2,1,0:T(2,128)S(1)} copy-done((s32[1,2,3]{2,1,0:T(2,128)S(1)}, s32[1,2,3]{2,1,0:T(2,128)}, u32[]{:S(2)}) %copy-start.6) | copy-done | bytes 48
  11.3 1.6 %gather_fusion = bf16[6,128,128]{2,1,0:T(8,128)(2,1)S(1)} fusion(bf16[16,128,128]{2,1,0:T(8,128)(2,1)} %param.14, s32[1024]{0:T(1024)S(1)} %pad_clamp_fusion.4), kind=kCustom, calls=%fused_computation | custom fusion | bytes 393240 | tf_op jit(solution)/shard_map/gather | solution.py:58
  13.0 0.1 broadcast_multiply_fusion
  13.1 0.6 %gather_fusion.1 = bf16[2,3,128,128]{3,2,1,0:T(8,128)(2,1)S(1)} fusion(bf16[2,3,128,128]{3,2,1,0:T(8,128)(2,1)S(1)} %broadcast_multiply_fusion, s32[1024]{0:T(1024)S(1)} %pad_clamp_fusion.3), kind=kCustom, calls=%fused_computation.1 | custom fusion | bytes 393224 | tf_op jit(solution)/shard_map/gather | solution.py:79
  13.7 0.0 collective-permute-done
  13.7 0.0 collective-permute-done.1
  13.8 0.0 collective-permute-done.2
  13.8 0.6 %gather_fusion.5 = bf16[6,2,128,128]{3,2,1,0:T(8,128)(2,1)S(1)} fusion(bf16[2,2,128,128]{3,2,1,0:T(8,128)(2,1)S(1)} %bitcast.76, s32[1024]{0:T(1024)S(1)} %pad_clamp_fusion), kind=kCustom, calls=%fused_computation.5 | custom fusion | bytes 786456 | tf_op jit(solution)/shard_map/gather | solution.py:77
  14.4 0.2 fusion.3
  14.7 5.3 %collective-permute-start.3 = (bf16[2,64,128]{2,1,0:T(8,128)(2,1)S(1)}, bf16[2,64,128]{2,1,0:T(8,128)(2,1)S(1)}, u32[]{:S(2)}, u32[]{:S(2)}) collective-permute-start(bf16[2,64,128]{2,1,0:T(8,128)(2,1)S(1)} %get-tuple-element.7), channel_id=1, source_target_pairs={{0,4},{4,8},{8,12},{1,5},{5,9},{9,13},{2,6},{6,10},{10,14},{3,7},{... | collective-permute-start | bytes 98312 | tf_op jit(solution)/shard_map/ppermute | solution.py:13
  20.0 1.9 %collective-permute-start.4 = (bf16[2,64,128]{2,1,0:T(8,128)(2,1)S(1)}, bf16[2,64,128]{2,1,0:T(8,128)(2,1)S(1)}, u32[]{:S(2)}, u32[]{:S(2)}) collective-permute-start(bf16[2,64,128]{2,1,0:T(8,128)(2,1)S(1)} %get-tuple-element.8), channel_id=1, source_target_pairs={{4,0},{8,4},{12,8},{5,1},{9,5},{13,9},{6,2},{10,6},{14,10},{7,3},{... | collective-permute-start | bytes 98312 | tf_op jit(solution)/shard_map/ppermute | solution.py:13
  21.9 0.0 collective-permute-done.3
  21.9 3.3 %collective-permute-done.4 = bf16[2,64,128]{2,1,0:T(8,128)(2,1)S(1)} collective-permute-done((bf16[2,64,128]{2,1,0:T(8,128)(2,1)S(1)}, bf16[2,64,128]{2,1,0:T(8,128)(2,1)S(1)}, u32[]{:S(2)}, u32[]{:S(2)}) %collective-permute-start.4) | collective-permute-done | bytes 32800 | tf_op jit(solution)/shard_map/ppermute | solution.py:13
  25.2 0.1 fusion.8
  25.3 0.7 %maximum_bitcast_fusion = bf16[1,2,256,128]{3,2,1,0:T(8,128)(2,1)} fusion(bf16[2,64,128]{2,1,0:T(8,128)(2,1)S(1)} %get-tuple-element.6, bf16[2,128,128]{2,1,0:T(8,128)(2,1)S(1)} %slice.26, bf16[2,64,128]{2,1,0:T(8,128)(2,1)S(1)} %get-tuple-element.5), kind=kLoop, calls=%fused_computation.17 | loop fusion | flops 393216 | bytes 262144 | tf_op jit(solution)/shard_map/broadcast_in_dim | solution.py:84
  (21 shorter events, 0.2 us)
Async XLA Ops:
  0.0 3.5 %copy-start = (bf16[16,128,128]{2,1,0:T(8,128)(2,1)S(1)}, bf16[16,128,128]{2,1,0:T(8,128)(2,1)}, u32[]{:S(2)}) copy-start(bf16[16,128,128]{2,1,0:T(8,128)(2,1)} %param.10) | copy-start | bytes 1572868
  1.0 0.7 %copy-start.3 = (s32[1,4,3]{1,0,2:T(1,128)S(1)}, s32[1,4,3]{1,0,2:T(1,128)}, u32[]{:S(2)}) copy-start(s32[1,4,3]{1,0,2:T(1,128)} %param.11) | copy-start | bytes 148
  1.0 0.7 %copy-start.4 = (s32[1,4,3]{1,0,2:T(1,128)S(1)}, s32[1,4,3]{1,0,2:T(1,128)}, u32[]{:S(2)}) copy-start(s32[1,4,3]{1,0,2:T(1,128)} %param.12) | copy-start | bytes 148
  2.1 0.7 %copy-start.2 = (s32[1,4,3]{1,0,2:T(1,128)S(1)}, s32[1,4,3]{1,0,2:T(1,128)}, u32[]{:S(2)}) copy-start(s32[1,4,3]{1,0,2:T(1,128)} %param.13) | copy-start | bytes 148
  4.6 9.1 %collective-permute-start = (bf16[2,64,128]{2,1,0:T(8,128)(2,1)S(1)}, bf16[2,64,128]{2,1,0:T(8,128)(2,1)S(1)}, u32[]{:S(2)}, u32[]{:S(2)}) collective-permute-start(bf16[2,64,128]{2,1,0:T(8,128)(2,1)S(1)} %get-tuple-element.11), channel_id=1, source_target_pairs={{0,1},{1,0},{2,3},{3,2},{4,5},{5,4},{6,7},{7,6},{8,9},{9,8},{10,11... | collective-permute-start | bytes 98312 | tf_op jit(solution)/shard_map/ppermute | solution.py:72
  6.8 6.9 %collective-permute-start.1 = (bf16[2,64,128]{2,1,0:T(8,128)(2,1)S(1)}, bf16[2,64,128]{2,1,0:T(8,128)(2,1)S(1)}, u32[]{:S(2)}, u32[]{:S(2)}) collective-permute-start(bf16[2,64,128]{2,1,0:T(8,128)(2,1)S(1)} %get-tuple-element.10), channel_id=1, source_target_pairs={{0,2},{1,3},{2,0},{3,1},{4,6},{5,7},{6,4},{7,5},{8,10},{9,11},{10,... | collective-permute-start | bytes 98312 | tf_op jit(solution)/shard_map/ppermute | solution.py:72
  9.1 4.7 %collective-permute-start.2 = (bf16[2,64,128]{2,1,0:T(8,128)(2,1)S(1)}, bf16[2,64,128]{2,1,0:T(8,128)(2,1)S(1)}, u32[]{:S(2)}, u32[]{:S(2)}) collective-permute-start(bf16[2,64,128]{2,1,0:T(8,128)(2,1)S(1)} %get-tuple-element.9), channel_id=1, source_target_pairs={{0,3},{1,2},{2,1},{3,0},{4,7},{5,6},{6,5},{7,4},{8,11},{9,10},{10,... | collective-permute-start | bytes 98312 | tf_op jit(solution)/shard_map/ppermute | solution.py:72
  9.1 0.7 %copy-start.1 = (s32[1,2,3]{2,1,0:T(2,128)S(1)}, s32[1,2,3]{2,1,0:T(2,128)}, u32[]{:S(2)}) copy-start(s32[1,2,3]{2,1,0:T(2,128)} %param.15) | copy-start | bytes 76
  9.8 0.7 %copy-start.5 = (s32[1,2,3]{2,1,0:T(2,128)S(1)}, s32[1,2,3]{2,1,0:T(2,128)}, u32[]{:S(2)}) copy-start(s32[1,2,3]{2,1,0:T(2,128)} %param.16) | copy-start | bytes 76
  10.7 0.7 %copy-start.6 = (s32[1,2,3]{2,1,0:T(2,128)S(1)}, s32[1,2,3]{2,1,0:T(2,128)}, u32[]{:S(2)}) copy-start(s32[1,2,3]{2,1,0:T(2,128)} %param.17) | copy-start | bytes 76
  14.7 7.2 %collective-permute-start.3 = (bf16[2,64,128]{2,1,0:T(8,128)(2,1)S(1)}, bf16[2,64,128]{2,1,0:T(8,128)(2,1)S(1)}, u32[]{:S(2)}, u32[]{:S(2)}) collective-permute-start(bf16[2,64,128]{2,1,0:T(8,128)(2,1)S(1)} %get-tuple-element.7), channel_id=1, source_target_pairs={{0,4},{4,8},{8,12},{1,5},{5,9},{9,13},{2,6},{6,10},{10,14},{3,7},{... | collective-permute-start | bytes 98312 | tf_op jit(solution)/shard_map/ppermute | solution.py:13
  20.0 5.2 %collective-permute-start.4 = (bf16[2,64,128]{2,1,0:T(8,128)(2,1)S(1)}, bf16[2,64,128]{2,1,0:T(8,128)(2,1)S(1)}, u32[]{:S(2)}, u32[]{:S(2)}) collective-permute-start(bf16[2,64,128]{2,1,0:T(8,128)(2,1)S(1)} %get-tuple-element.8), channel_id=1, source_target_pairs={{4,0},{8,4},{12,8},{5,1},{9,5},{13,9},{6,2},{10,6},{14,10},{7,3},{... | collective-permute-start | bytes 98312 | tf_op jit(solution)/shard_map/ppermute | solution.py:13
